TPU v7x, 256 devices: a whole 4x4x8 slice. The times are simulated.
256 devices in a mesh: seq: 32 (over x_hi, z, core), tensor: 8 (over x_lo, y).
Axes of the slice: x: 4 (x_hi: 2, x_lo: 2; x = x_hi * 2 + x_lo), y: 4, z: 8, core: 2. Of those that a mesh axis runs over, the one named last changes fastest.
Arguments:
- hidden: bfloat16 [8192, 2304], P('seq', 'tensor'), may hold values from -6 to 6
- attn_gain: float32 [2304], replicated, may hold values from 0.1 to 1.9
- query_weight: bfloat16 [2304, 2048], P(None, 'tensor'), may hold values from -1 to 1
- kv_weight: bfloat16 [2304, 2048], P(None, 'tensor'), may hold values from -1 to 1
- out_weight: bfloat16 [2048, 2304], P('tensor'), may hold values from -0.125 to 0.125
- post_gain: float32 [2304], replicated, may hold values from 0.1 to 1.9
- ff_gain: float32 [2304], replicated, may hold values from 0.1 to 1.9
- ff_post_gain: float32 [2304], replicated, may hold values from 0.1 to 1.9
- gate_weight: bfloat16 [2304, 9216], P('seq', 'tensor'), may hold values from -0.125 to 0.125
- up_weight: bfloat16 [2304, 9216], P('seq', 'tensor'), may hold values from -0.125 to 0.125
- down_weight_t: bfloat16 [2304, 9216], P('seq', 'tensor'), may hold values from -0.0625 to 0.0625
- next_gain: float32 [2304], replicated, may hold values from 0.1 to 1.9
- next_query_weight: bfloat16 [2304, 2048], P(None, 'tensor'), may hold values from -0.125 to 0.125
- next_kv_weight: bfloat16 [2304, 2048], P(None, 'tensor'), may hold values from -0.125 to 0.125
- lengths: int32 [4], replicated, may hold values from 256 to 3840, as said below
- pair_owner: int32 [32], replicated, may hold values from 0 to 31, each once
- page_table: int32 [64], replicated, may hold values from 0 to 63, each once
Outputs:
- hidden_out: bfloat16 [8192, 2304], P('seq', 'tensor')
- next_query: bfloat16 [8192, 2048], P('seq', 'tensor')
- next_kv: bfloat16 [8192, 2048], P('seq', 'tensor')
- kv_pages: bfloat16 [64, 128, 2048], P('seq', None, 'tensor')
Inputs may be any that keep to these rules, and one draw needn't show every extreme that they name: Four positive lengths summing to 8192; the first is the longest and the fourth the shortest. `pair_owner`: each mirrored pair b, the blocks b and 63 - b, is held by exactly one index of seq. `page_table`: every page takes exactly one block.
All inputs are finite; a program needn't handle non-finite values.
Results may differ from a plain program's by a relative error of at most 0.018.
Values may be sent and summed in bfloat16 or wider, within the bound.
A program may use at most 128 MiB of HBM per device.

v0:
```python
import jax
import jax.numpy as jnp
from jax import lax
from jax.sharding import PartitionSpec as P

EPS = 1e-06
SOFT_CAP = 50.0


def partner_2(block, axis, apart):
    count = lax.axis_size(axis)
    route = []
    for low in range(count):
        high = low | 1 << apart
        if high != low and high < count:
            route += [(low, high), (high, low)]
    return lax.ppermute(block, axis, route)


def row_norm(values, gain_vec):
    values = values.astype(jnp.float32)
    scale_vec = lax.rsqrt(jnp.mean(values * values, axis=-1, keepdims=True) + EPS)
    return values * scale_vec * gain_vec


def rotate(values, positions):
    half_dim = values.shape[-1] // 2
    freq_vec = 10000.0 ** (-jnp.arange(half_dim, dtype=jnp.float32) / half_dim)
    angles = positions.astype(jnp.float32)[:, None] * freq_vec[None, :]
    cosine_val = jnp.cos(angles)
    sine_val = jnp.sin(angles)
    leading = values[:, :half_dim]
    trailing = values[:, half_dim:]
    return jnp.concatenate(
        [leading * cosine_val - trailing * sine_val, trailing * cosine_val + leading * sine_val],
        axis=1,
    )


def tenant_of(stream_index, lengths):
    tenant_ends = jnp.cumsum(lengths)
    tenant_starts = tenant_ends - lengths
    tenant = jnp.sum((stream_index[:, None] >= tenant_ends[None, :3]).astype(jnp.int32), axis=1)
    selector = tenant[:, None] == jnp.arange(4, dtype=jnp.int32)[None, :]
    offset = jnp.sum(jnp.where(selector, tenant_starts[None, :], 0), axis=1)
    return (tenant, (stream_index - offset).astype(jnp.int32))


def body(
    hidden,
    attn_gain,
    query_weight,
    kv_weight,
    out_weight,
    post_gain,
    ff_gain,
    ff_post_gain,
    gate_weight,
    up_weight,
    down_weight_t,
    next_gain,
    next_query_weight,
    next_kv_weight,
    lengths,
    pair_owner,
    page_table,
):
    seq_count = lax.axis_size("seq")
    seq_index = lax.axis_index("seq")
    tensor_index = lax.axis_index("tensor")
    rows = hidden.shape[0]
    rows_half = rows // 2
    share = hidden.shape[1]
    head_dim = query_weight.shape[1]
    is_key = tensor_index % 2 == 0
    owned_pair = jnp.sum(
        jnp.where(jnp.arange(seq_count, dtype=jnp.int32) == seq_index, pair_owner, 0)
    )
    local_range = jnp.arange(rows_half, dtype=jnp.int32)
    tags = jnp.concatenate(
        [
            owned_pair * rows_half + local_range,
            (2 * seq_count - 1 - owned_pair) * rows_half + local_range,
        ]
    )
    tenant, position = tenant_of(tags, lengths)
    block_ids = jnp.arange(2 * seq_count, dtype=jnp.int32)
    page_blocks = [
        jnp.sum(jnp.where(page_table == 2 * seq_index + slot_index, block_ids, 0))
        for slot_index in range(2)
    ]
    wanted_tags = jnp.concatenate(
        [page_blocks[0] * rows_half + local_range, page_blocks[1] * rows_half + local_range]
    )
    full_hidden = lax.all_gather(hidden, "tensor", axis=1, tiled=True)
    attn_input = row_norm(full_hidden, attn_gain).astype(jnp.bfloat16)
    queries = rotate(
        jnp.dot(attn_input, query_weight, preferred_element_type=jnp.float32), position
    ).astype(jnp.bfloat16)
    own_proj = jnp.dot(attn_input, kv_weight, preferred_element_type=jnp.float32)
    own_part = jnp.where(is_key, rotate(own_proj, position), own_proj).astype(jnp.bfloat16)
    query_scale = head_dim ** (-0.5)
    partner = partner_2(own_part, "tensor", 0)
    key_mine = jnp.where(is_key, own_part, partner)
    value_mine = jnp.where(is_key, partner, own_part)
    key_rows = lax.all_gather(key_mine, "seq", axis=0, tiled=True)
    value_rows = lax.all_gather(value_mine, "seq", axis=0, tiled=True)
    key_tags = lax.all_gather(tags, "seq", axis=0, tiled=True)
    key_tenant, key_position = tenant_of(key_tags, lengths)
    allowed = (tenant[:, None] == key_tenant[None, :]) & (key_tags[None, :] <= tags[:, None])
    raw_scores = (
        lax.dot_general(
            queries, key_rows, (((1,), (1,)), ((), ())), preferred_element_type=jnp.float32
        )
        * query_scale
    )
    capped = SOFT_CAP * jnp.tanh(raw_scores / SOFT_CAP)
    weights = jnp.where(allowed, jnp.exp(capped), 0.0).astype(jnp.bfloat16)
    own_rows = jnp.where(is_key, key_rows, value_rows)
    numerator = jnp.dot(weights, value_rows, preferred_element_type=jnp.float32)
    denominator = jnp.sum(weights.astype(jnp.float32), axis=1)
    picker = (wanted_tags[:, None] == key_tags[None, :]).astype(jnp.bfloat16)
    cache_acc = jnp.dot(picker, own_rows, preferred_element_type=jnp.float32)
    attended = (numerator / denominator[:, None]).astype(jnp.bfloat16)
    attn_partial = jnp.dot(attended, out_weight, preferred_element_type=jnp.float32)
    column_start = tensor_index * share
    attn_sum = lax.psum(attn_partial, "tensor")
    middle = (full_hidden.astype(jnp.float32) + row_norm(attn_sum, post_gain)).astype(jnp.bfloat16)
    ff_input = row_norm(middle, ff_gain).astype(jnp.bfloat16)
    gate_val = jnp.dot(
        ff_input,
        lax.all_gather(gate_weight, "seq", axis=0, tiled=True),
        preferred_element_type=jnp.float32,
    )
    up_val = jnp.dot(
        ff_input,
        lax.all_gather(up_weight, "seq", axis=0, tiled=True),
        preferred_element_type=jnp.float32,
    )
    inner = (jax.nn.gelu(gate_val, approximate=True) * up_val).astype(jnp.bfloat16)
    ff_partial = lax.dot_general(
        inner,
        lax.all_gather(down_weight_t, "seq", axis=0, tiled=True),
        (((1,), (1,)), ((), ())),
        preferred_element_type=jnp.float32,
    )
    ff_sum = lax.psum(ff_partial.astype(jnp.bfloat16), "tensor").astype(jnp.float32)
    final_rows = (middle.astype(jnp.float32) + row_norm(ff_sum, ff_post_gain)).astype(jnp.bfloat16)
    next_input = row_norm(final_rows, next_gain).astype(jnp.bfloat16)
    hidden_out = lax.dynamic_slice_in_dim(final_rows, column_start, share, 1)
    next_query = rotate(
        jnp.dot(next_input, next_query_weight, preferred_element_type=jnp.float32), position
    ).astype(jnp.bfloat16)
    next_proj = jnp.dot(next_input, next_kv_weight, preferred_element_type=jnp.float32)
    next_kv = jnp.where(is_key, rotate(next_proj, position), next_proj).astype(jnp.bfloat16)
    kv_pages = cache_acc.astype(jnp.bfloat16).reshape(2, rows_half, head_dim)
    return (hidden_out, next_query, next_kv, kv_pages)


def solution(mesh):
    in_specs = (
        P("seq", "tensor"),
        P(),
        P(None, "tensor"),
        P(None, "tensor"),
        P("tensor", None),
        P(),
        P(),
        P(),
        P("seq", "tensor"),
        P("seq", "tensor"),
        P("seq", "tensor"),
        P(),
        P(None, "tensor"),
        P(None, "tensor"),
        P(),
        P(),
        P(),
    )
    out_specs = (
        P("seq", "tensor"),
        P("seq", "tensor"),
        P("seq", "tensor"),
        P("seq", None, "tensor"),
    )
    return jax.shard_map(body, mesh=mesh, in_specs=in_specs, out_specs=out_specs, check_vma=False)
```

profile of v0, /device:TPU:4, one launch (start us, length us, event | category | flops | bytes accessed | tf_op | source)
XLA Modules:
  0.0 710.7 jit_solution(15065292437494655086)
XLA Ops:
  8.0 1.3 fusion.89
  10.6 0.8 reduce-window.4
  12.3 41.9 %all-gather.8.cloned.1.call-done = bf16[256,2304]{0,1:T(8,128)(2,1)} async-done(((bf16[256,288]{0,1:T(8,128)(2,1)}), bf16[256,2304]{0,1:T(8,128)(2,1)}) %all-gather.8.cloned.1.call-update) | async-done | bytes 1179664 | tf_op jit(solution)/shard_map/all_gather | solution.py:95
  54.2 1.6 copy.29
  56.1 2.0 fusion.47
  58.9 5.0 collective-permute-done
  65.4 40.0 %all-gather = s32[32,1,256]{2,1,0:T(1,128)S(1)} all-gather(s32[1,1,256]{2,1,0:T(1,128)S(1)} %bitcast.22), channel_id=1, replica_groups=mesh['seq'=32,'tensor'=8] {'seq'}, dimensions={0}, use_global_device_ids=true | all-gather | bytes 33792 | tf_op jit(solution)/shard_map/all_gather | solution.py:108
  105.5 2.0 fusion.49
  108.1 40.5 %all-gather.10.cloned.1.call-done = bf16[8192,256]{0,1:T(8,128)(2,1)} async-done(((bf16[256,256]{0,1:T(8,128)(2,1)}), bf16[8192,256]{0,1:T(8,128)(2,1)}) %all-gather.10.cloned.1.call-update) | async-done | bytes 4194320 | tf_op jit(solution)/shard_map/all_gather | solution.py:106
  148.7 7.5 %convert_reduce_fusion = (f32[256]{0:T(256)S(1)}, bf16[256,8192]{1,0:T(8,128)(2,1)}) fusion(bf16[8192,256]{0,1:T(8,128)(2,1)} %all-gather.10.cloned.1.call-done, bf16[256,128]{0,1:T(8,128)(2,1)S(1)} %get-tuple-element.27, bf16[256,128]{0,1:T(8,128)(2,1)S(1)} %get-tuple-element.26, s32[256]{0:T(256)S(1)} %pad_add_fusion, s32[8192]{0:T(1024)S(1)} %bitcast.20, ...), kind=kOutput, calls=%fused_computation.6 | convolution fusion | flops 1092878080 | bytes 8588288 | tf_op jit(solution)/shard_map/dot_general | solution.py:112
  156.1 79.5 %all-gather.12.cloned.1.call-done = bf16[8192,256]{0,1:T(8,128)(2,1)} async-done(((bf16[256,256]{0,1:T(8,128)(2,1)}), bf16[8192,256]{0,1:T(8,128)(2,1)}) %all-gather.12.cloned.1.call-update) | async-done | bytes 4194320 | tf_op jit(solution)/shard_map/all_gather | solution.py:107
  235.6 7.2 %fusion.38 = f32[256,2304]{1,0:T(8,128)} fusion(bf16[256,2304]{1,0:T(8,128)(2,1)S(1)} %copy-done, bf16[256,8192]{1,0:T(8,128)(2,1)} %get-tuple-element.33, bf16[8192,256]{0,1:T(8,128)(2,1)} %all-gather.12.cloned.1.call-done, f32[256]{0:T(256)S(1)} %get-tuple-element.32), kind=kOutput, calls=%fused_computation.51 | convolution fusion | flops 1375862784 | bytes 11928576 | tf_op jit(solution)/shard_map/dot_general | solution.py:125
  245.0 86.2 %all-reduce.3.cloned.1.call-done = f32[256,2304]{1,0:T(8,128)} async-done(((f32[256,2304]{1,0:T(8,128)}), f32[256,2304]{1,0:T(8,128)}) %all-reduce.3.cloned.1.call-update) | async-done | bytes 2359312 | tf_op jit(solution)/shard_map/psum | solution.py:127
  331.2 2.1 multiply_reduce_fusion
  334.3 88.3 %all-gather.14.cloned.1.call-done = bf16[2304,1152]{1,0:T(8,128)(2,1)} async-done(((bf16[72,1152]{1,0:T(8,128)(2,1)}), bf16[2304,1152]{1,0:T(8,128)(2,1)}) %all-gather.14.cloned.1.call-update) | async-done | bytes 5308432 | tf_op jit(solution)/shard_map/all_gather | solution.py:132
  422.6 5.4 fusion.45
  427.9 84.7 %all-gather.16.cloned.1.call-done = bf16[2304,1152]{1,0:T(8,128)(2,1)} async-done(((bf16[72,1152]{1,0:T(8,128)(2,1)}), bf16[2304,1152]{1,0:T(8,128)(2,1)}) %all-gather.16.cloned.1.call-update) | async-done | bytes 5308432 | tf_op jit(solution)/shard_map/all_gather | solution.py:137
  512.7 90.3 %all-gather.18.cloned.1.call-done = bf16[2304,1152]{1,0:T(8,128)(2,1)} async-done(((bf16[72,1152]{1,0:T(8,128)(2,1)}), bf16[2304,1152]{1,0:T(8,128)(2,1)}) %all-gather.18.cloned.1.call-update) | async-done | bytes 5308432 | tf_op jit(solution)/shard_map/all_gather | solution.py:143
  602.9 8.8 %convolution_convert_fusion = bf16[256,2304]{1,0:T(8,128)(2,1)} fusion(bf16[2304,1152]{1,0:T(8,128)(2,1)} %all-gather.18.cloned.1.call-done, bf16[2304,1152]{1,0:T(8,128)(2,1)} %all-gather.16.cloned.1.call-done, f32[256,1152]{1,0:T(8,128)} %fusion.45, bf16[256,2304]{1,0:T(8,128)(2,1)S(1)} %get-tuple-element.21, f32[2304]{0:T(1024)S(1)} %copy-done.11, ...), kind=kOutput, calls=%fused_computation.13 | convolution fusion | flops 2723807232 | bytes 14166016 | tf_op jit(solution)/shard_map/dot_general | solution.py:141
  613.8 4.4 fusion.32
  618.2 75.5 %all-reduce.5.cloned.1.call-done = bf16[256,2304]{1,0:T(8,128)(2,1)} async-done(((bf16[256,2304]{1,0:T(8,128)(2,1)}), bf16[256,2304]{1,0:T(8,128)(2,1)}) %all-reduce.5.cloned.1.call-update) | async-done | bytes 1179664 | tf_op jit(solution)/shard_map/psum | solution.py:147
  693.7 1.7 fusion.12
  695.4 2.0 fusion.14
  699.6 2.0 fusion.53
  (77 shorter events, 13.1 us)
Async XLA Ops:
  7.2 228.4 %copy-start = (bf16[256,2304]{1,0:T(8,128)(2,1)S(1)}, bf16[256,2304]{1,0:T(8,128)(2,1)}, u32[]{:S(2)}) copy-start(bf16[256,2304]{1,0:T(8,128)(2,1)} %param.21) | copy-start | bytes 3538948
  7.2 49.0 %copy-start.10 = (f32[2304]{0:T(1024)S(1)}, f32[2304]{0:T(1024)}, u32[]{:S(2)}) copy-start(f32[2304]{0:T(1024)} %param.18) | copy-start | bytes 27652
  7.2 47.0 %all-gather.8.cloned.1.call-start = ((), (), s32[]{:S(2)}) async-start(), calls=%async_computation | async-start | bytes 1327104 | tf_op jit(solution)/shard_map/all_gather | solution.py:95
  7.9 140.7 %all-gather.10.cloned.1.call-start = ((), (), s32[]{:S(2)}) async-start(), calls=%async_computation.1 | async-start | bytes 4325376 | tf_op jit(solution)/shard_map/all_gather | solution.py:106
  11.4 96.1 %copy-start.6 = (f32[128]{0:T(128)}, f32[128]{0:T(128)S(1)}, u32[]{:S(2)}) copy-start(f32[128]{0:T(128)S(1)} %multiply_power_fusion) | copy-start | bytes 1540
  58.8 5.1 collective-permute-start
  64.6 171.0 %all-gather.12.cloned.1.call-start = ((), (), s32[]{:S(2)}) async-start(), calls=%async_computation.2 | async-start | bytes 4325376 | tf_op jit(solution)/shard_map/all_gather | solution.py:107
  65.3 265.9 %all-reduce.3.cloned.1.call-start = ((), (), s32[]{:S(2)}) async-start(), calls=%async_computation.3 | async-start | bytes 4718592 | tf_op jit(solution)/shard_map/psum | solution.py:127
  105.4 50.8 %copy-start.2 = (s32[32,1,256]{2,1,0:T(1,128)}, s32[32,1,256]{2,1,0:T(1,128)S(1)}, u32[]{:S(2)}) copy-start(s32[32,1,256]{2,1,0:T(1,128)S(1)} %all-gather) | copy-start | bytes 98308
  242.8 90.4 %copy-start.4 = (f32[2304]{0:T(1024)S(1)}, f32[2304]{0:T(1024)}, u32[]{:S(2)}) copy-start(f32[2304]{0:T(1024)} %param.22) | copy-start | bytes 27652
  242.9 179.7 %all-gather.14.cloned.1.call-start = ((), (), s32[]{:S(2)}) async-start(), calls=%async_computation.4 | async-start | bytes 5474304 | tf_op jit(solution)/shard_map/all_gather | solution.py:132
  243.5 269.2 %all-gather.16.cloned.1.call-start = ((), (), s32[]{:S(2)}) async-start(), calls=%async_computation.5 | async-start | bytes 5474304 | tf_op jit(solution)/shard_map/all_gather | solution.py:137
  244.0 358.9 %all-gather.18.cloned.1.call-start = ((), (), s32[]{:S(2)}) async-start(), calls=%async_computation.6 | async-start | bytes 5474304 | tf_op jit(solution)/shard_map/all_gather | solution.py:143
  244.8 448.9 %all-reduce.5.cloned.1.call-start = ((), (), s32[]{:S(2)}) async-start(), calls=%async_computation.7 | async-start | bytes 2359296 | tf_op jit(solution)/shard_map/psum | solution.py:147
  331.2 2.4 copy-start.1
  422.6 180.4 %copy-start.11 = (f32[2304]{0:T(1024)S(1)}, f32[2304]{0:T(1024)}, u32[]{:S(2)}) copy-start(f32[2304]{0:T(1024)} %param.23) | copy-start | bytes 27652
  427.9 183.9 %copy-start.8 = (s32[64]{0:T(128)S(1)}, s32[64]{0:T(128)}, u32[]{:S(2)}) copy-start(s32[64]{0:T(128)} %param.33) | copy-start | bytes 772
  427.9 185.8 %copy-start.3 = (s32[32,1,256]{2,1,0:T(1,128)S(1)}, s32[32,1,256]{2,1,0:T(1,128)}, u32[]{:S(2)}) copy-start(s32[32,1,256]{2,1,0:T(1,128)} %copy-done.2) | copy-start | bytes 98308
  613.8 81.6 %copy-start.5 = (f32[2304]{0:T(1024)S(1)}, f32[2304]{0:T(1024)}, u32[]{:S(2)}) copy-start(f32[2304]{0:T(1024)} %param.24) | copy-start | bytes 27652
  693.7 3.7 copy-start.9
  693.7 3.7 copy-start.12
  697.4 0.8 copy-start.7
  697.4 2.2 copy-start.13
Sparse Core Ops, SparseCore 0:
  9.8 44.3 all-gather.7
  64.7 83.9 all-gather.9
  151.8 83.7 all-gather.11
  243.0 88.1 all-reduce.2
  333.7 88.7 all-gather.13
  425.1 87.5 all-gather.15
  515.4 87.5 all-gather.17
  611.9 81.7 all-reduce.4
where the time goes:
time: 711 us
  waiting for transfers between devices  595 us (84%)
  matrix products  40.1 us (6%)
  blocking collectives  40 us (6%)
  between operations  17 us (2%)
  other arithmetic  13.6 us (2%)
    all_gather x1, waiting for transfers between devices, body(): lax.all_gather(down_weight_t, 'seq', axis=0, tiled=True)  90.3 us
    all_gather x1, waiting for transfers between devices, body(): lax.all_gather(gate_weight, 'seq', axis=0, tiled=True)  88.3 us
    psum x1, waiting for transfers between devices, body(): attn_sum = lax.psum(attn_partial, 'tensor')  86.2 us
    all_gather x1, waiting for transfers between devices, body(): lax.all_gather(up_weight, 'seq', axis=0, tiled=True)  84.7 us
    all_gather x1, waiting for transfers between devices, body(): value_rows = lax.all_gather(value_mine, 'seq', axis=0, tiled=True)  79.5 us
    psum x1, waiting for transfers between devices, body(): lax.psum(ff_partial.astype(jnp.bfloat16), 'tensor').astype(jnp.float32)  75.5 us
    all_gather x1, waiting for transfers between devices, body(): full_hidden = lax.all_gather(hidden, 'tensor', axis=1, tiled=True)  41.9 us
    all_gather x1, waiting for transfers between devices, body(): key_rows = lax.all_gather(key_mine, 'seq', axis=0, tiled=True)  40.5 us
  transfers between devices with their start and end apart: 9, of which 9 were waited for; matrix products, arithmetic and copies ran while one was open for 4% of the time, Pallas kernels for 0%

commit v1 on v0

--- a/solution.py
+++ b/solution.py
@@ -5,6 +5,13 @@
 
 EPS = 1e-06
 SOFT_CAP = 50.0
+
+
+def all_by_exchange(value, mesh_axis, dim):
+    count = lax.axis_size(mesh_axis)
+    parts = jnp.stack([value for _ in range(count)])
+    parts = lax.all_to_all(parts, mesh_axis, split_axis=0, concat_axis=0)
+    return jnp.concatenate(parts, axis=dim)
 
 
 def partner_2(block, axis, apart):
@@ -133,9 +140,7 @@
         preferred_element_type=jnp.float32,
     )
     up_val = jnp.dot(
-        ff_input,
-        lax.all_gather(up_weight, "seq", axis=0, tiled=True),
-        preferred_element_type=jnp.float32,
+        ff_input, all_by_exchange(up_weight, "seq", 0), preferred_element_type=jnp.float32
     )
     inner = (jax.nn.gelu(gate_val, approximate=True) * up_val).astype(jnp.bfloat16)
     ff_partial = lax.dot_general(

time: 711 us -> 659 us (0.927)
  waiting for transfers between devices: 595 us -> 532 us
  starting transfers between devices: 0.58 us -> 8.09 us
    all_gather x1 -> x0, waiting for transfers between devices: 84.7 us -> none  [body(): lax.all_gather(up_weight, 'seq', axis=0, tiled=True)]
    psum x1, waiting for transfers between devices: 86.2 us -> 112 us  [body(): attn_sum = lax.psum(attn_partial, 'tensor')]
    all_to_all x0 -> x1, starting transfers between devices: none -> 7.54 us  [all_by_exchange(): parts = lax.all_to_all(parts, mesh_axis, split_axis=0, concat_axis=0)]
  transfers between devices with their start and end apart: 9 -> 9, of which waited for: 9 -> 8; matrix products, arithmetic and copies ran while one was open for 4% -> 4% of each run, Pallas kernels for 0% -> 0%
where the time goes in v1:
time: 659 us; the launch traced here: 658 us
  waiting for transfers between devices  532 us (81%)
  matrix products  40 us (6%)
  blocking collectives  40 us (6%)
  between operations  17 us (3%)
  other arithmetic  13.6 us (2%)
  starting transfers between devices  8.09 us (1%)
  local copies, waits for them, and re-layouts  7.31 us (1%)
    psum x1, waiting for transfers between devices, body(): attn_sum = lax.psum(attn_partial, 'tensor')  112 us
    all_gather x1, waiting for transfers between devices, body(): lax.all_gather(gate_weight, 'seq', axis=0, tiled=True)  90.3 us
    all_gather x1, waiting for transfers between devices, body(): lax.all_gather(down_weight_t, 'seq', axis=0, tiled=True)  84.8 us
    all_gather x1, waiting for transfers between devices, body(): value_rows = lax.all_gather(value_mine, 'seq', axis=0, tiled=True)  79.5 us
    psum x1, waiting for transfers between devices, body(): lax.psum(ff_partial.astype(jnp.bfloat16), 'tensor').astype(jnp.float32)  75.5 us
    all_gather x1, waiting for transfers between devices, body(): full_hidden = lax.all_gather(hidden, 'tensor', axis=1, tiled=True)  41.9 us
    all_gather x1, waiting for transfers between devices, body(): key_rows = lax.all_gather(key_mine, 'seq', axis=0, tiled=True)  40.5 us
    all_gather x1, blocking collectives, body(): key_tags = lax.all_gather(tags, 'seq', axis=0, tiled=True)  40 us
  transfers between devices with their start and end apart: 9, of which 8 were waited for; matrix products, arithmetic and copies ran while one was open for 4% of the time, Pallas kernels for 0%

profile of v1, /device:TPU:4, one launch (start us, length us, event | category | flops | bytes accessed | tf_op | source)
XLA Modules:
  0.0 658.0 jit_solution(14095452790835733)
XLA Ops:
  8.0 1.3 fusion.89
  12.3 41.9 %all-gather.7.cloned.1.call-done = bf16[256,2304]{0,1:T(8,128)(2,1)} async-done(((bf16[256,288]{0,1:T(8,128)(2,1)}), bf16[256,2304]{0,1:T(8,128)(2,1)}) %all-gather.7.cloned.1.call-update) | async-done | bytes 1179664 | tf_op jit(solution)/shard_map/all_gather | solution.py:102
  54.2 1.6 copy.29
  56.1 2.0 fusion.47
  58.9 5.0 collective-permute-done
  65.4 40.0 %all-gather = s32[32,1,256]{2,1,0:T(1,128)S(1)} all-gather(s32[1,1,256]{2,1,0:T(1,128)S(1)} %bitcast.23), channel_id=1, replica_groups=mesh['seq'=32,'tensor'=8] {'seq'}, dimensions={0}, use_global_device_ids=true | all-gather | bytes 33792 | tf_op jit(solution)/shard_map/all_gather | solution.py:115
  105.5 2.0 fusion.49
  108.1 40.5 %all-gather.9.cloned.1.call-done = bf16[8192,256]{0,1:T(8,128)(2,1)} async-done(((bf16[256,256]{0,1:T(8,128)(2,1)}), bf16[8192,256]{0,1:T(8,128)(2,1)}) %all-gather.9.cloned.1.call-update) | async-done | bytes 4194320 | tf_op jit(solution)/shard_map/all_gather | solution.py:113
  148.7 7.5 %convert_reduce_fusion = (f32[256]{0:T(256)S(1)}, bf16[256,8192]{1,0:T(8,128)(2,1)}) fusion(bf16[8192,256]{0,1:T(8,128)(2,1)} %all-gather.9.cloned.1.call-done, bf16[256,128]{0,1:T(8,128)(2,1)S(1)} %get-tuple-element.27, bf16[256,128]{0,1:T(8,128)(2,1)S(1)} %get-tuple-element.26, s32[256]{0:T(256)S(1)} %pad_add_fusion, s32[8192]{0:T(1024)S(1)} %bitcast.21, ...), kind=kOutput, calls=%fused_computation.6 | convolution fusion | flops 1092878080 | bytes 8588288 | tf_op jit(solution)/shard_map/dot_general | solution.py:119
  156.1 79.5 %all-gather.11.cloned.1.call-done = bf16[8192,256]{0,1:T(8,128)(2,1)} async-done(((bf16[256,256]{0,1:T(8,128)(2,1)}), bf16[8192,256]{0,1:T(8,128)(2,1)}) %all-gather.11.cloned.1.call-update) | async-done | bytes 4194320 | tf_op jit(solution)/shard_map/all_gather | solution.py:114
  235.6 7.2 %fusion.38 = f32[256,2304]{1,0:T(8,128)} fusion(bf16[256,2304]{1,0:T(8,128)(2,1)S(1)} %copy-done, bf16[256,8192]{1,0:T(8,128)(2,1)} %get-tuple-element.33, bf16[8192,256]{0,1:T(8,128)(2,1)} %all-gather.11.cloned.1.call-done, f32[256]{0:T(256)S(1)} %get-tuple-element.32), kind=kOutput, calls=%fused_computation.51 | convolution fusion | flops 1375862784 | bytes 11928576 | tf_op jit(solution)/shard_map/dot_general | solution.py:132
  243.7 2.6 stack.2
  246.3 7.5 %all-to-all-start = ((bf16[32,72,1152]{2,1,0:T(8,128)(2,1)}), bf16[32,72,1152]{2,1,0:T(8,128)(2,1)}, u32[]{:S(2)}, u32[]{:S(2)}) async-start(bf16[32,72,1152]{2,1,0:T(8,128)(2,1)} %stack.2), calls=%async_computation | async-start | bytes 10616832 | tf_op jit(solution)/shard_map/all_to_all | solution.py:13
  254.7 112.0 %all-reduce.3.cloned.1.call-done = f32[256,2304]{1,0:T(8,128)} async-done(((f32[256,2304]{1,0:T(8,128)}), f32[256,2304]{1,0:T(8,128)}) %all-reduce.3.cloned.1.call-update) | async-done | bytes 2359312 | tf_op jit(solution)/shard_map/psum | solution.py:134
  366.7 2.1 multiply_reduce_fusion
  369.7 90.3 %all-gather.13.cloned.1.call-done = bf16[2304,1152]{1,0:T(8,128)(2,1)} async-done(((bf16[72,1152]{1,0:T(8,128)(2,1)}), bf16[2304,1152]{1,0:T(8,128)(2,1)}) %all-gather.13.cloned.1.call-update) | async-done | bytes 5308432 | tf_op jit(solution)/shard_map/all_gather | solution.py:139
  460.1 5.3 fusion.45
  465.4 84.8 %all-gather.15.cloned.1.call-done = bf16[2304,1152]{1,0:T(8,128)(2,1)} async-done(((bf16[72,1152]{1,0:T(8,128)(2,1)}), bf16[2304,1152]{1,0:T(8,128)(2,1)}) %all-gather.15.cloned.1.call-update) | async-done | bytes 5308432 | tf_op jit(solution)/shard_map/all_gather | solution.py:148
  550.2 8.9 %convolution_convert_fusion = bf16[256,2304]{1,0:T(8,128)(2,1)} fusion(bf16[2304,1152]{1,0:T(8,128)(2,1)} %all-gather.15.cloned.1.call-done, bf16[2304,1152]{1,0:T(8,128)(2,1)} %bitcast.5, f32[256,1152]{1,0:T(8,128)} %fusion.45, bf16[256,2304]{1,0:T(8,128)(2,1)S(1)} %get-tuple-element.21, f32[2304]{0:T(1024)S(1)} %copy-done.12, f32[256]{0:T(256)S(1)} %add_rsqrt_fusion.2), kind=kOutput, calls=%fused_computation.13 | convolution fusion | flops 2723807232 | bytes 14166016 | tf_op jit(solution)/shard_map/dot_general | solution.py:146
  561.1 4.4 fusion.32
  565.5 75.5 %all-reduce.5.cloned.1.call-done = bf16[256,2304]{1,0:T(8,128)(2,1)} async-done(((bf16[256,2304]{1,0:T(8,128)(2,1)}), bf16[256,2304]{1,0:T(8,128)(2,1)}) %all-reduce.5.cloned.1.call-update) | async-done | bytes 1179664 | tf_op jit(solution)/shard_map/psum | solution.py:152
  641.0 1.7 fusion.12
  642.7 2.0 fusion.14
  646.9 2.0 fusion.53
  (79 shorter events, 13.5 us)
Async XLA Ops:
  7.2 228.4 %copy-start = (bf16[256,2304]{1,0:T(8,128)(2,1)S(1)}, bf16[256,2304]{1,0:T(8,128)(2,1)}, u32[]{:S(2)}) copy-start(bf16[256,2304]{1,0:T(8,128)(2,1)} %param.21) | copy-start | bytes 3538948
  7.2 49.0 %copy-start.11 = (f32[2304]{0:T(1024)S(1)}, f32[2304]{0:T(1024)}, u32[]{:S(2)}) copy-start(f32[2304]{0:T(1024)} %param.18) | copy-start | bytes 27652
  7.2 47.0 %all-gather.7.cloned.1.call-start = ((), (), s32[]{:S(2)}) async-start(), calls=%async_computation.1 | async-start | bytes 1327104 | tf_op jit(solution)/shard_map/all_gather | solution.py:102
  7.9 140.7 %all-gather.9.cloned.1.call-start = ((), (), s32[]{:S(2)}) async-start(), calls=%async_computation.2 | async-start | bytes 4325376 | tf_op jit(solution)/shard_map/all_gather | solution.py:113
  11.4 96.1 %copy-start.7 = (f32[128]{0:T(128)}, f32[128]{0:T(128)S(1)}, u32[]{:S(2)}) copy-start(f32[128]{0:T(128)S(1)} %multiply_power_fusion) | copy-start | bytes 1540
  58.8 5.1 collective-permute-start
  64.6 171.0 %all-gather.11.cloned.1.call-start = ((), (), s32[]{:S(2)}) async-start(), calls=%async_computation.3 | async-start | bytes 4325376 | tf_op jit(solution)/shard_map/all_gather | solution.py:114
  65.3 301.4 %all-reduce.3.cloned.1.call-start = ((), (), s32[]{:S(2)}) async-start(), calls=%async_computation.4 | async-start | bytes 4718592 | tf_op jit(solution)/shard_map/psum | solution.py:134
  105.4 50.8 %copy-start.3 = (s32[32,1,256]{2,1,0:T(1,128)}, s32[32,1,256]{2,1,0:T(1,128)S(1)}, u32[]{:S(2)}) copy-start(s32[32,1,256]{2,1,0:T(1,128)S(1)} %all-gather) | copy-start | bytes 98308
  242.8 0.9 copy-start.2
  242.8 217.3 %all-gather.13.cloned.1.call-start = ((), (), s32[]{:S(2)}) async-start(), calls=%async_computation.5 | async-start | bytes 5474304 | tf_op jit(solution)/shard_map/all_gather | solution.py:139
  246.3 219.1 %all-to-all-start = ((bf16[32,72,1152]{2,1,0:T(8,128)(2,1)}), bf16[32,72,1152]{2,1,0:T(8,128)(2,1)}, u32[]{:S(2)}, u32[]{:S(2)}) async-start(bf16[32,72,1152]{2,1,0:T(8,128)(2,1)} %stack.2), calls=%async_computation | async-start | bytes 10616832 | tf_op jit(solution)/shard_map/all_to_all | solution.py:13
  253.9 114.9 %copy-start.5 = (f32[2304]{0:T(1024)S(1)}, f32[2304]{0:T(1024)}, u32[]{:S(2)}) copy-start(f32[2304]{0:T(1024)} %param.22) | copy-start | bytes 27652
  253.9 296.3 %all-gather.15.cloned.1.call-start = ((), (), s32[]{:S(2)}) async-start(), calls=%async_computation.6 | async-start | bytes 5474304 | tf_op jit(solution)/shard_map/all_gather | solution.py:148
  254.5 386.5 %all-reduce.5.cloned.1.call-start = ((), (), s32[]{:S(2)}) async-start(), calls=%async_computation.7 | async-start | bytes 2359296 | tf_op jit(solution)/shard_map/psum | solution.py:152
  366.7 2.4 copy-start.1
  460.1 90.1 %copy-start.12 = (f32[2304]{0:T(1024)S(1)}, f32[2304]{0:T(1024)}, u32[]{:S(2)}) copy-start(f32[2304]{0:T(1024)} %param.23) | copy-start | bytes 27652
  550.2 8.9 %copy-start.9 = (s32[64]{0:T(128)S(1)}, s32[64]{0:T(128)}, u32[]{:S(2)}) copy-start(s32[64]{0:T(128)} %param.33) | copy-start | bytes 772
  550.2 10.9 %copy-start.4 = (s32[32,1,256]{2,1,0:T(1,128)S(1)}, s32[32,1,256]{2,1,0:T(1,128)}, u32[]{:S(2)}) copy-start(s32[32,1,256]{2,1,0:T(1,128)} %copy-done.3) | copy-start | bytes 98308
  561.1 81.6 %copy-start.6 = (f32[2304]{0:T(1024)S(1)}, f32[2304]{0:T(1024)}, u32[]{:S(2)}) copy-start(f32[2304]{0:T(1024)} %param.24) | copy-start | bytes 27652
  641.0 3.7 copy-start.10
  641.0 3.7 copy-start.13
  644.7 0.8 copy-start.8
  644.7 2.2 copy-start.14
Sparse Core Ops, SparseCore 0:
  9.8 44.3 all-gather.6
  64.7 83.9 all-gather.8
  151.8 83.7 all-gather.10
  242.9 123.7 all-reduce.2
  369.2 90.8 all-gather.12
  462.6 87.5 all-gather.14
  559.2 81.7 all-reduce.4
